TPU v7x, 512 devices: a whole 4x4x16 slice. The times are simulated.
512 devices in a mesh: tok: 16 (over z), scol: 4 (over y), tcol: 8 (over x, core).
Axes of the slice: x: 4, y: 4, z: 16, core: 2. Of those that a mesh axis runs over, the one named last changes fastest.
Arguments:
- student: float32 [8192, 4096], P('tok', 'scol'), may hold values from -6 to 6
- teacher: float32 [8192, 4096], P('tok', 'tcol'), may hold values from -6 to 6
- teacher_norm: float32 [1], replicated, may hold values from 262144 to 1048576
Outputs:
- student_grad: float32 [8192, 4096], P(('tok', 'tcol'), 'scol')
All inputs are finite; a program needn't handle non-finite values.
Results may differ from a plain program's by a relative error of at most 0.000073.
Values sent between devices are 32-bit elements; how exact they have to be, the bound alone decides.
A program may use at most 64 MiB of HBM per device.

v0:
```python
import jax
import jax.numpy as jnp
from jax import lax
from jax.sharding import PartitionSpec as P

DS = 4096


def token_contract(left, right):
    return lax.dot_general(
        left,
        right,
        (((0,), (0,)), ((), ())),
        precision=lax.Precision.HIGHEST,
        preferred_element_type=jnp.float32,
    )


def feature_contract(left, right):
    return lax.dot_general(
        left,
        right,
        (((1,), (1,)), ((), ())),
        precision=lax.Precision.HIGHEST,
        preferred_element_type=jnp.float32,
    )


def body(student, teacher, teacher_norm):
    col_index = lax.axis_index("tcol")
    tcol_count = lax.axis_size("tcol")
    tok_rows = student.shape[0]
    all_columns = lax.all_gather(student, "scol", axis=1, tiled=True)
    block_width = all_columns.shape[1] // tcol_count
    partner = lax.dynamic_slice_in_dim(all_columns, col_index * block_width, block_width, 1)
    cov_block = token_contract(student, teacher)
    gram_block = token_contract(student, partner)
    cov_block, gram_block = lax.psum((cov_block, gram_block), "tok")
    local_stats = jnp.stack([jnp.sum(cov_block * cov_block), jnp.sum(gram_block * gram_block)])
    gathered = lax.all_gather(local_stats, ("scol", "tcol"), axis=0, tiled=True)
    totals = jnp.sum(gathered.reshape(-1, 2), axis=0)
    tokens_all = tok_rows * lax.axis_size("tok")
    factor = -2.0 * tokens_all * DS / (jnp.sqrt(totals[1]) * teacher_norm[0])
    gram_ratio = totals[0] / totals[1]
    result = feature_contract(teacher, cov_block) - gram_ratio * feature_contract(
        partner, gram_block
    )
    return lax.psum_scatter(factor * result, "tcol", scatter_dimension=0, tiled=True)


def solution(mesh):
    return jax.shard_map(
        body,
        mesh=mesh,
        in_specs=(P("tok", "scol"), P("tok", "tcol"), P()),
        out_specs=P(("tok", "tcol"), "scol"),
        check_vma=False,
    )
```

profile of v0, /device:TPU:1, one launch (start us, length us, event | category | flops | bytes accessed | tf_op | source)
XLA Modules:
  0.0 388.7 jit_solution(13710487400168556864)
XLA Ops:
  6.5 0.0 copy-start
  6.5 0.0 copy-start.1
  6.5 0.0 all-gather.2.cloned.1.call-start
  6.5 0.7 all-gather.2.cloned.1.call-update
  7.3 0.0 all-reduce.4.cloned.1.call-start
  7.3 0.4 copy-done
  7.8 0.7 copy-done.1
  8.5 4.8 %fusion.7 = f32[1024,512]{1,0:T(8,128)} fusion(f32[512,1024]{1,0:T(8,128)S(1)} %copy-done.1, f32[512,512]{1,0:T(8,128)S(1)} %copy-done), kind=kOutput, calls=%fused_computation.12 | convolution fusion | flops 3221225472 | bytes 5242880 | tf_op jit(solution)/shard_map/dot_general | solution.py:10
  13.3 92.1 %all-gather.2.cloned.1.call-done = f32[512,4096]{1,0:T(8,128)} async-done(((f32[512,1024]{1,0:T(8,128)}), f32[512,4096]{1,0:T(8,128)}) %all-gather.2.cloned.1.call-update) | async-done | bytes 8388624 | tf_op jit(solution)/shard_map/all_gather | solution.py:33
  105.4 6.1 %convolution_bitcast_fusion = f32[1024,512]{0,1:T(8,128)} fusion(f32[512,1024]{1,0:T(8,128)S(1)} %copy-done.1, f32[512,4096]{1,0:T(8,128)} %all-gather.2.cloned.1.call-done, s32[]{:T(128)S(6)} %select_n.3), kind=kOutput, calls=%fused_computation.4 | convolution fusion | flops 3221225472 | bytes 5242884 | tf_op jit(solution)/shard_map/dot_general | solution.py:10
  111.4 0.0 all-reduce.4.cloned.1.call-update
  111.5 0.0 reduce-scatter.4.cloned.1.call-start
  112.2 1.3 dynamic-slice
  114.1 146.2 %all-reduce.4.cloned.1.call-done = (f32[1024,512]{0,1:T(8,128)}, f32[1024,512]{1,0:T(8,128)}) async-done(((f32[1024,512]{0,1:T(8,128)}, f32[1024,512]{1,0:T(8,128)}), (f32[1024,512]{0,1:T(8,128)}, f32[1024,512]{1,0:T(8,128)})) %all-reduce.4.cloned.1.call-update) | async-done | bytes 4194320 | tf_op jit(solution)/shard_map/psum | solution.py:38
  260.3 0.0 copy-start.2
  260.3 2.9 multiply_reduce_fusion.1
  263.2 0.0 copy-done.2
  263.2 1.2 multiply_reduce_fusion
  264.4 1.4 maximum_dynamic-update-slice_fusion
  265.9 71.9 %all-reduce = f32[64]{0:T(128)S(1)} all-reduce(f32[64]{0:T(128)S(1)} %maximum_dynamic-update-slice_fusion), channel_id=1, replica_groups=mesh['tok'=16,'scol'=4,'tcol'=8] {'scol','tcol'}, use_global_device_ids=true, to_apply=%add | all-reduce | flops 64 | bytes 512
  337.8 0.1 reshape.8
  337.9 0.6 fusion.6
  340.6 0.0 copy-start.3
  340.6 4.9 %fusion.1 = f32[512,1024]{0,1:T(8,128)S(1)} fusion(f32[1024,512]{0,1:T(8,128)S(1)} %copy-done.2, f32[512,4096]{1,0:T(8,128)} %all-gather.2.cloned.1.call-done, s32[]{:T(128)S(6)} %select_n.3), kind=kOutput, calls=%fused_computation.5 | convolution fusion | flops 3221225472 | bytes 5242884 | tf_op jit(solution)/shard_map/dot_general | solution.py:20
  345.5 0.0 copy-done.3
  345.5 3.6 fusion
  349.1 1.9 copy.11
  351.0 0.0 reduce-scatter.4.cloned.1.call-update
  351.0 31.2 %reduce-scatter.4.cloned.1.call-done = f32[64,1024]{1,0:T(8,128)} async-done(((f32[512,1024]{1,0:T(8,128)}), f32[64,1024]{1,0:T(8,128)}) %reduce-scatter.4.cloned.1.call-update) | async-done | bytes 262160 | tf_op jit(solution)/shard_map/reduce_scatter | solution.py:48
  (2 shorter events, 0.0 us)
Async XLA Ops:
  6.5 1.2 copy-start
  6.5 1.9 copy-start.1
  6.5 98.8 %all-gather.2.cloned.1.call-start = ((), (), s32[]{:S(2)}) async-start(), calls=%async_computation.1 | async-start | bytes 10485760 | tf_op jit(solution)/shard_map/all_gather | solution.py:33
  7.3 253.1 %all-reduce.4.cloned.1.call-start = ((), (), s32[]{:S(2)}) async-start(), calls=%async_computation.3 | async-start | bytes 8388608 | tf_op jit(solution)/shard_map/psum | solution.py:38
  111.5 270.8 %reduce-scatter.4.cloned.1.call-start = ((), (), s32[]{:S(2)}) async-start(), calls=%async_computation.2 | async-start | bytes 2359296 | tf_op jit(solution)/shard_map/reduce_scatter | solution.py:48
  260.3 2.9 copy-start.2
  340.6 4.9 %copy-start.3 = (f32[1024,512]{1,0:T(8,128)S(1)}, f32[1024,512]{1,0:T(8,128)}, u32[]{:S(2)}) copy-start(f32[1024,512]{1,0:T(8,128)} %get-tuple-element.6) | copy-start | bytes 6291460
Sparse Core Ops, SparseCore 0:
  9.4 95.8 all-gather.1
  111.6 148.6 all-reduce.3
  351.2 31.0 reduce-scatter.3
where the time goes:
time: 390 us; the launch traced here: 389 us
  waiting for transfers between devices  270 us (69%)
  blocking collectives  71.9 us (18%)
  matrix products  19.3 us (5%)
  between operations  16.6 us (4%)
  other arithmetic  5.57 us (1%)
  local copies, waits for them, and re-layouts  4.99 us (1%)
    psum x1, waiting for transfers between devices, body(): cov_block, gram_block = lax.psum((cov_block, gram_block), 'tok')  146 us
    all_gather x1, waiting for transfers between devices, body(): all_columns = lax.all_gather(student, 'scol', axis=1, tiled=True)  92.1 us
    unnamed x1, blocking collectives  71.9 us
    reduce_scatter x1, waiting for transfers between devices, body(): lax.psum_scatter(factor * result, 'tcol', scatter_dimension=0, tiled=True)  31.2 us
    dot_general x2, matrix products, token_contract(): lax.dot_general(left, right, (((0,), (0,)), ((), ())), precision=lax.Prec...  10.9 us
    dot_general x2, matrix products, feature_contract(): lax.dot_general(left, right, (((1,), (1,)), ((), ())), precision=lax.Prec...  8.48 us
  transfers between devices with their start and end apart: 3, of which 3 were waited for; matrix products, arithmetic and copies ran while one was open for 2% of the time, Pallas kernels for 0%

commit v1 on v0

v1 whole, which is shorter than its diff:
```python
import functools

import jax
import jax.numpy as jnp
from jax import lax
from jax.experimental import pallas as pl
from jax.experimental.pallas import tpu as pltpu
from jax.sharding import PartitionSpec as P

DS = 4096
TOKENS = 8192
MESH = pl.DeviceIdType.MESH
NZ = 16
TOK = 512
SC = 1024
TC = 512
CH = SC // NZ
KS = 4
KR = CH // KS
PW = 2 * CH
NP = SC // PW
OT = TOK // 8


def split(value):
    high = value.astype(jnp.bfloat16)
    return high, (value - high.astype(jnp.float32)).astype(jnp.bfloat16)


def dot3(ah, al, bh, bl, dims):
    def one(a, b):
        return lax.dot_general(a, b, (dims, ((), ())), preferred_element_type=jnp.float32)

    return one(ah, bh) + (one(ah, bl) + one(al, bh))


def kernel(
    s_ref,
    t_ref,
    tn_ref,
    out_ref,
    st_hi,
    st_lo,
    ab_hi,
    ab_lo,
    yq,
    pbuf,
    own,
    rbuf,
    full,
    opair,
    cx,
    qbuf,
    xrecv,
    stat,
    pstat,
    cstat,
    xstat,
    ystat,
    rs_send,
    rs_recv,
    ag_send,
    ag_recv,
    y_send,
    y_recv,
    p_send,
    p_recv,
    st_send,
    st_recv,
    pl_send,
    pl_recv,
    a_send,
    a_recv,
    b_send,
    b_recv,
):
    z = lax.axis_index("tok")
    y = lax.axis_index("scol")
    j = lax.axis_index("tcol")
    x = j // 2
    c = j % 2
    zdev = ({"tok": (z + 1) % NZ}, {"tok": (z + NZ - 1) % NZ})
    ydev = [{"scol": (y + d) % 4} for d in (1, 2, 3)]
    xdev = [{"tcol": ((x + d) % 4) * 2 + c} for d in (1, 2, 3)]
    sib = {"tcol": 2 * x + 1 - c}

    barrier = pltpu.get_barrier_semaphore()
    for dev in (*zdev, *ydev, *xdev, sib):
        pl.semaphore_signal(barrier, inc=1, device_id=dev, device_id_type=MESH)

    def rcopy(src, dst, ssem, rsem, dev):
        return pltpu.make_async_remote_copy(
            src_ref=src, dst_ref=dst, send_sem=ssem, recv_sem=rsem, device_id=dev, device_id_type=MESH
        )

    def rows(o, k):
        return pl.ds(pl.multiple_of(o * CH + k * KR, KR), KR)

    def rs_first(ph, d, k):
        o = (z + 8) % NZ
        return rcopy(
            own.at[ph, rows(o, k)],
            rbuf.at[ph, d, 0, pl.ds(k * KR, KR)],
            rs_send.at[ph, d, 0, k],
            rs_recv.at[ph, d, 0, k],
            zdev[d],
        )

    def rs_copy(ph, d, s, k):
        return rcopy(
            rbuf.at[ph, d, s - 2, pl.ds(k * KR, KR)],
            rbuf.at[ph, d, s - 1, pl.ds(k * KR, KR)],
            rs_send.at[ph, d, s - 1, k],
            rs_recv.at[ph, d, s - 1, k],
            zdev[d],
        )

    def rs_wait(ph, d, s, k):
        rcopy(
            rbuf.at[ph, d, s - 1, pl.ds(k * KR, KR)],
            rbuf.at[ph, d, s - 1, pl.ds(k * KR, KR)],
            rs_send.at[ph, d, s - 1, k],
            rs_recv.at[ph, d, s - 1, k],
            zdev[d],
        ).wait_recv()

    def main(d, k):
        return (k < KS // 2) if d == 0 else (k >= KS // 2)

    def rs_start(ph):
        for k in range(KS):
            rs_first(ph, 0 if k < KS // 2 else 1, k).start()

    def rs_step(ph, s):
        offs = ((z + 9 - s) % NZ, (z + s + 7) % NZ)
        for k in range(KS):
            for d in (0, 1):
                here = (ph, d, s - 2, pl.ds(k * KR, KR))
                mine = own[ph, rows(offs[d], k)]
                if main(d, k):
                    rs_wait(ph, d, s - 1, k)
                    rbuf[here] = rbuf[here] + mine
                else:

                    @pl.when(s > 2)
                    def _():
                        rs_wait(ph, d, s - 1, k)
                        rbuf[here] = rbuf[here] + mine

                    @pl.when(s == 2)
                    def _():
                        rbuf[here] = mine

                rs_copy(ph, d, s, k).start()

    def rs_final(ph):
        total = jnp.zeros((8, 128), jnp.float32)
        for k in range(KS):
            for d in (0, 1):
                rs_wait(ph, d, 8, k)
            at = pl.ds(k * KR, KR)
            value = own[ph, rows(z, k)] + (rbuf[ph, 0, 7, at] + rbuf[ph, 1, 7, at])
            full[ph, rows(z, k)] = value
            square = value * value
            for a in range(0, KR, 8):
                for b in range(0, TC, 128):
                    total = total + square[a : a + 8, b : b + 128]
        return total

    def ag_copy(ph, d, t, k):
        o = (z + NZ + 1 - t) % NZ if d == 0 else (z + t - 1) % NZ
        return rcopy(
            full.at[ph, rows(o, k)],
            full.at[ph, rows(o, k)],
            ag_send.at[ph, d, t - 1, k],
            ag_recv.at[ph, d, t - 1, k],
            zdev[d],
        )

    def ag_wait(ph, d, t, k):
        o = (z + NZ - t) % NZ if d == 0 else (z + t) % NZ
        rcopy(
            full.at[ph, rows(o, k)],
            full.at[ph, rows(o, k)],
            ag_send.at[ph, d, t - 1, k],
            ag_recv.at[ph, d, t - 1, k],
            zdev[d],
        ).wait_recv()

    def ag_start(ph):
        for k in range(KS):
            for d in (0, 1):
                ag_copy(ph, d, 1, k).start()

    def ag_arrive(ph, t):
        for k in range(KS):
            for d in (0, 1):
                last = 7 if main(d, k) else 6

                @pl.when(t <= last + 1)
                def _():
                    ag_wait(ph, d, t, k)

                @pl.when(t <= last)
                def _():
                    ag_copy(ph, d, t + 1, k).start()

    def products(ph, o1, o2):
        r1 = pl.ds(pl.multiple_of(o1 * CH, CH), CH)
        r2 = pl.ds(pl.multiple_of(o2 * CH, CH), CH)
        lh = jnp.concatenate([st_hi[r1], st_hi[r2]], axis=0)
        ll = jnp.concatenate([st_lo[r1], st_lo[r2]], axis=0)
        value = dot3(lh, ll, ab_hi[ph], ab_lo[ph], ((1,), (0,)))
        own[ph, r1] = value[:CH]
        own[ph, r2] = value[CH:]

    def products_at(ph, s):
        products(ph, (z + 9 - s) % NZ, (z + s + 7) % NZ)

    def pair_of(t):
        up = (z + t) % 2
        return ((up * (z + t - 1) + (1 - up) * (z + NZ - t)) % NZ) // 2

    def pair_product(ph, t):
        p = pair_of(t)
        wh, wl = split(full[ph, pl.ds(pl.multiple_of(p * PW, PW), PW)])
        value = dot3(ab_hi[ph], ab_lo[ph], wh, wl, ((1,), (1,)))
        return value.reshape(4, 2, OT, PW)

    def stat_copy(d, t):
        o = (z + NZ + 1 - t) % NZ if d == 0 else (z + t - 1) % NZ
        return rcopy(stat.at[o], stat.at[o], st_send.at[d, t - 1], st_recv.at[d, t - 1], zdev[d])

    def stat_wait(d, t):
        o = (z + NZ - t) % NZ if d == 0 else (z + t) % NZ
        rcopy(stat.at[o], stat.at[o], st_send.at[d, t - 1], st_recv.at[d, t - 1], zdev[d]).wait_recv()

    def plane_copy(i):
        if i == 0:
            return rcopy(pstat.at[0], cstat, pl_send.at[0], pl_recv.at[0], sib)
        if i < 4:
            return rcopy(pstat.at[1], xstat.at[i - 1], pl_send.at[i], pl_recv.at[i], xdev[i - 1])
        return rcopy(pstat.at[2], ystat.at[i - 4], pl_send.at[i], pl_recv.at[i], ydev[i - 4])

    def y_copy(d):
        return rcopy(
            s_ref.at[pl.ds(pl.multiple_of(x * 128, 128), 128), pl.ds(pl.multiple_of(c * TC, TC), TC)],
            yq.at[d - 1],
            y_send.at[d - 1],
            y_recv.at[d - 1],
            ydev[d - 1],
        )

    def p_copy(d, at):
        return rcopy(
            yq.at[d - 1],
            pbuf.at[pl.ds(pl.multiple_of(at * 128, 128), 128)],
            p_send.at[d - 1],
            p_recv.at[at],
            {"tcol": ((y + 4 - d) % 4) * 2 + c},
        )

    def forward(d):
        source = (y + 4 - d) % 4
        y_copy(d).wait_recv()

        @pl.when(source == x)
        def _():
            pbuf[pl.ds(pl.multiple_of(x * 128, 128), 128)] = yq[d - 1]

        @pl.when(source != x)
        def _():
            p_copy(d, x).start()

    def a_copy(q):
        return rcopy(opair.at[1, q - 1, :, 1 - c], cx.at[q - 1], a_send.at[q - 1], a_recv.at[q - 1], sib)

    def b_copy(q, d):
        return rcopy(
            qbuf.at[q - 1, (x + d) % 4],
            xrecv.at[d - 1, q - 1],
            b_send.at[d - 1, q - 1],
            b_recv.at[d - 1, q - 1],
            xdev[d - 1],
        )

    def stage_b(q):
        a_copy(q).wait_recv()
        qbuf[q - 1] = opair[1, q - 1, :, c] + cx[q - 1]
        for d in (1, 3, 2):
            b_copy(q, d).start()

    def stage_f(q):
        for d in (1, 2, 3):
            b_copy(q, d).wait_recv()
        value = (qbuf[q - 1, x] + xrecv[0, q - 1]) + (xrecv[1, q - 1] + xrecv[2, q - 1])
        p = pair_of(q)
        out_ref[:, pl.ds(pl.multiple_of(p * PW, PW), PW)] = value

    th, tl = split(t_ref[...])
    ab_hi[0] = th
    ab_lo[0] = tl
    for a in range(0, SC, 256):
        sh, sl = split(s_ref[:, a : a + 256].T)
        st_hi[a : a + 256] = sh
        st_lo[a : a + 256] = sl
    pl.semaphore_wait(barrier, 9)
    for d in (1, 3, 2):
        y_copy(d).start()

    products(0, (z + 8) % NZ, z)
    rs_start(0)

    @pl.loop(2, 9)
    def _(s):
        products_at(0, s)
        rs_step(0, s)

        @pl.when(s == 5)
        def _():
            forward(1)
            forward(3)

        @pl.when(s == 7)
        def _():
            forward(2)

    @pl.when(x == y)
    def _():
        pbuf[...] = s_ref[:, pl.ds(pl.multiple_of(c * TC, TC), TC)]

    @pl.when(x != y)
    def _():
        for e in (1, 2, 3):
            p_copy(1, (x + e) % 4).wait_recv()

    ph_, pl_ = split(pbuf[...])
    ab_hi[1] = ph_
    ab_lo[1] = pl_
    products(1, (z + 8) % NZ, z)
    rs_start(1)
    stat[z, :8] = rs_final(0)

    @pl.loop(2, 9)
    def _(s):
        products_at(1, s)
        rs_step(1, s)

    ag_start(0)
    stat[z, 8:] = rs_final(1)
    for d in (0, 1):
        stat_copy(d, 1).start()

    @pl.loop(1, 9)
    def _(t):
        @pl.when(t == 8)
        def _():
            ag_start(1)

        ag_arrive(0, t)
        for d in (0, 1):
            last = 8 if d == 0 else 7

            @pl.when(t <= last)
            def _():
                stat_wait(d, t)

            @pl.when(t < last)
            def _():
                stat_copy(d, t + 1).start()

        opair[0, t - 1] = pair_product(0, t)

    total = stat[0]
    for o in range(1, NZ):
        total = total + stat[o]
    pstat[0] = total
    plane_copy(0).start()

    @pl.loop(1, 9)
    def _(t):
        ag_arrive(1, t)
        opair[1, t - 1] = pair_product(1, t)

        @pl.when(t == 1)
        def _():
            plane_copy(0).wait_recv()
            pstat[1] = pstat[0] + cstat[...]
            for i in (1, 2, 3):
                plane_copy(i).start()

        @pl.when(t == 2)
        def _():
            for i in (1, 2, 3):
                plane_copy(i).wait_recv()
            pstat[2] = (pstat[1] + xstat[0]) + (xstat[1] + xstat[2])
            for i in (4, 5, 6):
                plane_copy(i).start()

        @pl.when(t == 3)
        def _():
            for i in (4, 5, 6):
                plane_copy(i).wait_recv()
            value = (pstat[2] + ystat[0]) + (ystat[1] + ystat[2])
            hsic = jnp.sum(value[:8], keepdims=True)
            gram_sq = jnp.sum(value[8:], keepdims=True)
            factor = -2.0 * TOKENS * DS / (jnp.sqrt(gram_sq) * tn_ref[0])
            ratio = hsic / gram_sq
            pstat[3, :8] = jnp.broadcast_to(factor, (8, 128))
            pstat[3, 8:] = jnp.broadcast_to(ratio, (8, 128))

        def finish(q):
            factor = pstat[3, 0:1]
            ratio = pstat[3, 8:9]
            opair[1, q - 1] = factor * (opair[0, q - 1] - ratio * opair[1, q - 1])
            a_copy(q).start()

        @pl.when(t == 4)
        def _():
            pl.loop(1, 4)(finish)

        @pl.when(t >= 4)
        def _():
            finish(t)

        @pl.when(t == 5)
        def _():
            pl.loop(1, 4)(stage_b)

        @pl.when(t >= 5)
        def _():
            stage_b(t - 1)

        @pl.when(t == 6)
        def _():
            pl.loop(1, 4)(stage_f)

        @pl.when(t >= 6)
        def _():
            stage_f(t - 2)

    stage_b(8)
    stage_f(7)
    stage_f(8)

    for d in (1, 2, 3):
        y_copy(d).wait_send()

        @pl.when((y + 4 - d) % 4 != x)
        def _():
            p_copy(d, x).wait_send()

    for ph in (0, 1):
        for k in range(KS):
            rs_first(ph, 0 if k < KS // 2 else 1, k).wait_send()

        @pl.loop(2, 9)
        def _(s):
            for k in range(KS):
                for d in (0, 1):
                    rs_copy(ph, d, s, k).wait_send()

        @pl.loop(1, 9)
        def _(t):
            for k in range(KS):
                for d in (0, 1):
                    last = 8 if main(d, k) else 7

                    @pl.when(t <= last)
                    def _():
                        ag_copy(ph, d, t, k).wait_send()

    @pl.loop(1, 9)
    def _(t):
        stat_copy(0, t).wait_send()

        @pl.when(t < 8)
        def _():
            stat_copy(1, t).wait_send()

        a_copy(t).wait_send()
        for d in (1, 2, 3):
            b_copy(t, d).wait_send()

    for i in range(7):
        plane_copy(i).wait_send()


def body(student, teacher, teacher_norm):
    f32, bf16 = jnp.float32, jnp.bfloat16
    dma = pltpu.SemaphoreType.DMA
    return pl.pallas_call(
        kernel,
        out_shape=jax.ShapeDtypeStruct((OT, SC), f32),
        in_specs=[
            pl.BlockSpec(memory_space=pltpu.VMEM),
            pl.BlockSpec(memory_space=pltpu.VMEM),
            pl.BlockSpec(memory_space=pltpu.SMEM),
        ],
        out_specs=pl.BlockSpec(memory_space=pltpu.VMEM),
        scratch_shapes=[
            pltpu.VMEM((SC, TOK), bf16),
            pltpu.VMEM((SC, TOK), bf16),
            pltpu.VMEM((2, TOK, TC), bf16),
            pltpu.VMEM((2, TOK, TC), bf16),
            pltpu.VMEM((3, 128, TC), f32),
            pltpu.VMEM((TOK, TC), f32),
            pltpu.VMEM((2, SC, TC), f32),
            pltpu.VMEM((2, 2, 8, CH, TC), f32),
            pltpu.VMEM((2, SC, TC), f32),
            pltpu.VMEM((2, NP, 4, 2, OT, PW), f32),
            pltpu.VMEM((NP, 4, OT, PW), f32),
            pltpu.VMEM((NP, 4, OT, PW), f32),
            pltpu.VMEM((3, NP, OT, PW), f32),
            pltpu.VMEM((NZ, 16, 128), f32),
            pltpu.VMEM((4, 16, 128), f32),
            pltpu.VMEM((16, 128), f32),
            pltpu.VMEM((3, 16, 128), f32),
            pltpu.VMEM((3, 16, 128), f32),
            dma((2, 2, 8, KS)),
            dma((2, 2, 8, KS)),
            dma((2, 2, 8, KS)),
            dma((2, 2, 8, KS)),
            dma((3,)),
            dma((3,)),
            dma((3,)),
            dma((4,)),
            dma((2, 8)),
            dma((2, 8)),
            dma((7,)),
            dma((7,)),
            dma((8,)),
            dma((8,)),
            dma((3, 8)),
            dma((3, 8)),
        ],
        compiler_params=pltpu.CompilerParams(
            collective_id=0, has_side_effects=True, vmem_limit_bytes=48 * 1024 * 1024
        ),
    )(student, teacher, teacher_norm)


def solution(mesh):
    return jax.shard_map(
        body,
        mesh=mesh,
        in_specs=(P("tok", "scol"), P("tok", "tcol"), P()),
        out_specs=P(("tok", "tcol"), "scol"),
        check_vma=False,
    )
```

time: 390 us -> 146 us (0.37)
  waiting for transfers between devices: 270 us -> 0 us
  Pallas kernels: 0 us -> 142 us
  blocking collectives: 71.9 us -> 0 us
  matrix products: 19.3 us -> 0 us
  between operations: 16.6 us -> 0.67 us
  other arithmetic: 5.57 us -> 0 us
    psum x1 -> x0, waiting for transfers between devices: 146 us -> none  [body(): cov_block, gram_block = lax.psum((cov_block, gram_block), 'tok')]
    pallas_call x0 -> x1, Pallas kernels: none -> 142 us  [body(): pl.pallas_call(kernel, out_shape=jax.ShapeDtypeStruct((OT, SC), f32), in_...]
    all_gather x1 -> x0, waiting for transfers between devices: 92.1 us -> none  [body(): all_columns = lax.all_gather(student, 'scol', axis=1, tiled=True)]
    unnamed x1 -> x0, blocking collectives: 71.9 us -> none
    reduce_scatter x1 -> x0, waiting for transfers between devices: 31.2 us -> none  [body(): lax.psum_scatter(factor * result, 'tcol', scatter_dimension=0, tiled=True)]
    dot_general x4 -> x0, matrix products: 19.3 us -> none  [the longest x2 10.9 us: token_contract(): lax.dot_general(left, right, (((0,), (0,)), ((), ())), precision=lax.Prec...]
    reduce_sum x3 -> x0, other arithmetic: 4.13 us -> none  [the longest x1 2.91 us: body(): jnp.sum(cov_block * cov_block)]
  transfers between devices with their start and end apart: 3 -> 0, of which waited for: 3 -> 0; matrix products, arithmetic and copies ran while one was open for 2% -> 0% of each run, Pallas kernels for 0% -> 0%
where the time goes in v1:
time: 146 us
  Pallas kernels  142 us (97%)
  local copies, waits for them, and re-layouts  3.51 us (2%)
    pallas_call x1, Pallas kernels, body(): pl.pallas_call(kernel, out_shape=jax.ShapeDtypeStruct((OT, SC), f32), in_...  142 us
    unnamed x5, local copies, waits for them, and re-layouts  3.51 us

profile of v1, /device:TPU:1, one launch (start us, length us, event | category | flops | bytes accessed | tf_op | source)
XLA Modules:
  0.0 145.8 jit_solution(2909298254400822182)
XLA Ops:
  0.7 0.0 copy-start
  0.7 1.6 %copy-done = f32[512,1024]{1,0:T(8,128)S(1)} copy-done((f32[512,1024]{1,0:T(8,128)S(1)}, f32[512,1024]{1,0:T(8,128)}, u32[]{:S(2)}) %copy-start) | copy-done | bytes 2097176
  2.2 0.0 copy-start.1
  2.2 1.2 copy-done.1
  3.5 141.7 %shard_map.37 = f32[64,1024]{1,0:T(8,128)S(1)} custom-call(f32[512,1024]{1,0:T(8,128)S(1)} %copy-done, f32[512,512]{1,0:T(8,128)S(1)} %copy-done.1, f32[1]{0:T(128)S(6)} %copy.5.tn_ref), custom_call_target="tpu_custom_call" | custom-call | tf_op jit(solution)/shard_map/pallas_call | solution.py:492
  145.1 0.7 copy.6
Async XLA Ops:
  0.7 1.6 %copy-start = (f32[512,1024]{1,0:T(8,128)S(1)}, f32[512,1024]{1,0:T(8,128)}, u32[]{:S(2)}) copy-start(f32[512,1024]{1,0:T(8,128)} %s_ref.1) | copy-start | bytes 6291460
  2.2 1.2 copy-start.1

commit v2 on v1

v2 whole, which is shorter than its diff:
```python
import functools

import jax
import jax.numpy as jnp
from jax import lax
from jax.experimental import pallas as pl
from jax.experimental.pallas import tpu as pltpu
from jax.sharding import PartitionSpec as P

DS = 4096
TOKENS = 8192
MESH = pl.DeviceIdType.MESH
NZ = 16
TOK = 512
SC = 1024
TC = 512
CH = SC // NZ
KS = 4
KR = CH // KS
PW = 2 * CH
NP = SC // PW
OT = TOK // 8


def split(value):
    high = value.astype(jnp.bfloat16)
    return high, (value - high.astype(jnp.float32)).astype(jnp.bfloat16)


def dot3(ah, al, bh, bl, dims):
    def one(a, b):
        return lax.dot_general(a, b, (dims, ((), ())), preferred_element_type=jnp.float32)

    return one(ah, bh) + (one(ah, bl) + one(al, bh))


def kernel(
    s_ref,
    t_ref,
    tn_ref,
    out_ref,
    st_hi,
    st_lo,
    ab_hi,
    ab_lo,
    yq,
    pbuf,
    own,
    rbuf,
    full,
    opair,
    cx,
    qbuf,
    xrecv,
    zstat,
    tstat,
    ystat,
    scale,
    rs_send,
    rs_recv,
    ag_send,
    ag_recv,
    y_send,
    y_recv,
    p_send,
    p_recv,
    st_send,
    st_recv,
    ts_send,
    ts_recv,
    ys_send,
    ys_recv,
    a_send,
    a_recv,
    b_send,
    b_recv,
):
    z = lax.axis_index("tok")
    y = lax.axis_index("scol")
    j = lax.axis_index("tcol")
    x = j // 2
    c = j % 2
    zdev = ({"tok": (z + 1) % NZ}, {"tok": (z + NZ - 1) % NZ})
    ydev = [{"scol": (y + d) % 4} for d in (1, 2, 3)]
    xdev = [{"tcol": ((x + d) % 4) * 2 + c} for d in (1, 2, 3)]
    sib = {"tcol": 2 * x + 1 - c}
    tdev = [{"tcol": (j + e) % 8} for e in range(1, 8)]

    barrier = pltpu.get_barrier_semaphore()
    for dev in (*zdev, *ydev, *tdev):
        pl.semaphore_signal(barrier, inc=1, device_id=dev, device_id_type=MESH)

    def rcopy(src, dst, ssem, rsem, dev):
        return pltpu.make_async_remote_copy(
            src_ref=src, dst_ref=dst, send_sem=ssem, recv_sem=rsem, device_id=dev, device_id_type=MESH
        )

    def rows(o, k):
        return pl.ds(pl.multiple_of(o * CH + k * KR, KR), KR)

    def rs_first(ph, d, k):
        o = (z + 8) % NZ
        return rcopy(
            own.at[ph, rows(o, k)],
            rbuf.at[ph, d, 0, pl.ds(k * KR, KR)],
            rs_send.at[ph, d, k],
            rs_recv.at[ph, d, 0, k],
            zdev[d],
        )

    def rs_copy(ph, d, s, k):
        return rcopy(
            rbuf.at[ph, d, s - 2, pl.ds(k * KR, KR)],
            rbuf.at[ph, d, s - 1, pl.ds(k * KR, KR)],
            rs_send.at[ph, d, k],
            rs_recv.at[ph, d, s - 1, k],
            zdev[d],
        )

    def rs_wait(ph, d, s, k):
        rcopy(
            rbuf.at[ph, d, s - 1, pl.ds(k * KR, KR)],
            rbuf.at[ph, d, s - 1, pl.ds(k * KR, KR)],
            rs_send.at[ph, d, k],
            rs_recv.at[ph, d, s - 1, k],
            zdev[d],
        ).wait_recv()

    def main(d, k):
        return (k < KS // 2) if d == 0 else (k >= KS // 2)

    def rs_second(ph, d, k):
        o = (z + 7) % NZ if d == 0 else (z + 9) % NZ
        return rcopy(
            own.at[ph, rows(o, k)],
            rbuf.at[ph, d, 1, pl.ds(k * KR, KR)],
            rs_send.at[ph, d, k],
            rs_recv.at[ph, d, 1, k],
            zdev[d],
        )

    def rs_start(ph):
        products(ph, (z + 8) % NZ, z)
        for k in range(KS):
            rs_first(ph, 0 if k < KS // 2 else 1, k).start()
        products_at(ph, 2)
        for k in range(KS):
            rs_second(ph, 1 if k < KS // 2 else 0, k).start()

    def rs_step(ph, s, only_main=False):
        offs = ((z + 9 - s) % NZ, (z + s + 7) % NZ)
        for k in range(KS):
            for d in (0, 1):
                if only_main and not main(d, k):
                    continue
                here = (ph, d, s - 2, pl.ds(k * KR, KR))
                mine = own[ph, rows(offs[d], k)]
                rs_wait(ph, d, s - 1, k)
                rbuf[here] = rbuf[here] + mine
                rs_copy(ph, d, s, k).start()

    def rs_final(ph):
        total = jnp.zeros((8, 128), jnp.float32)
        for k in range(KS):
            for d in (0, 1):
                rs_wait(ph, d, 8, k)
            at = pl.ds(k * KR, KR)
            value = own[ph, rows(z, k)] + (rbuf[ph, 0, 7, at] + rbuf[ph, 1, 7, at])
            full[ph, rows(z, k)] = value
            square = value * value
            for a in range(0, KR, 8):
                for b in range(0, TC, 128):
                    total = total + square[a : a + 8, b : b + 128]
        zstat[z, :, ph * 128 : ph * 128 + 128] = jnp.sum(total, axis=0, keepdims=True)

    def ag_copy(ph, d, t, k):
        o = (z + NZ + 1 - t) % NZ if d == 0 else (z + t - 1) % NZ
        return rcopy(
            full.at[ph, rows(o, k)],
            full.at[ph, rows(o, k)],
            ag_send.at[ph, d, k],
            ag_recv.at[ph, d, t - 1, k],
            zdev[d],
        )

    def ag_wait(ph, d, t, k):
        o = (z + NZ - t) % NZ if d == 0 else (z + t) % NZ
        rcopy(
            full.at[ph, rows(o, k)],
            full.at[ph, rows(o, k)],
            ag_send.at[ph, d, k],
            ag_recv.at[ph, d, t - 1, k],
            zdev[d],
        ).wait_recv()

    def ag_start(ph):
        for k in range(KS):
            for d in (0, 1):
                ag_copy(ph, d, 1, k).start()

    def ag_arrive(ph, t, last=6):
        for k in range(KS):
            for d in (0, 1):
                if last < 8 or main(d, k):
                    ag_wait(ph, d, t, k)
                if last < 7 or (last == 7 and main(d, k)):
                    ag_copy(ph, d, t + 1, k).start()

    def products(ph, o1, o2):
        r1 = pl.ds(pl.multiple_of(o1 * CH, CH), CH)
        r2 = pl.ds(pl.multiple_of(o2 * CH, CH), CH)
        lh = jnp.concatenate([st_hi[r1], st_hi[r2]], axis=0)
        ll = jnp.concatenate([st_lo[r1], st_lo[r2]], axis=0)
        value = dot3(lh, ll, ab_hi[ph], ab_lo[ph], ((1,), (0,)))
        own[ph, r1] = value[:CH]
        own[ph, r2] = value[CH:]

    def products_at(ph, s):
        products(ph, (z + 9 - s) % NZ, (z + s + 7) % NZ)

    def pair_of(t):
        up = (z + t) % 2
        return ((up * (z + t - 1) + (1 - up) * (z + NZ - t)) % NZ) // 2

    def pair_product(ph, t):
        p = pair_of(t)
        wh, wl = split(full[ph, pl.ds(pl.multiple_of(p * PW, PW), PW)])
        value = dot3(ab_hi[ph], ab_lo[ph], wh, wl, ((1,), (1,)))
        return value.reshape(4, 2, OT, PW)

    def zs_copy(e):
        return rcopy(zstat.at[z], zstat.at[z], st_send, st_recv, {"tok": (z + e) % NZ})

    def zs_all():
        part = zstat.at[pl.ds(0, NZ - 1)]
        return rcopy(part, part, st_send, st_recv, zdev[0])

    def ts_copy(e):
        return rcopy(tstat.at[j], tstat.at[j], ts_send, ts_recv, tdev[e - 1])

    def ts_all():
        part = tstat.at[pl.ds(0, 7)]
        return rcopy(part, part, ts_send, ts_recv, tdev[0])

    def ys_copy(e):
        return rcopy(ystat.at[y], ystat.at[y], ys_send, ys_recv, ydev[e - 1])

    def ys_all():
        part = ystat.at[pl.ds(0, 3)]
        return rcopy(part, part, ys_send, ys_recv, ydev[0])

    def y_copy(d):
        return rcopy(
            s_ref.at[pl.ds(pl.multiple_of(x * 128, 128), 128), pl.ds(pl.multiple_of(c * TC, TC), TC)],
            yq.at[d - 1],
            y_send.at[d - 1],
            y_recv.at[d - 1],
            ydev[d - 1],
        )

    def p_copy(d, at):
        return rcopy(
            yq.at[d - 1],
            pbuf.at[pl.ds(pl.multiple_of(at * 128, 128), 128)],
            p_send.at[d - 1],
            p_recv.at[at],
            {"tcol": ((y + 4 - d) % 4) * 2 + c},
        )

    def forward(d):
        source = (y + 4 - d) % 4
        y_copy(d).wait_recv()

        @pl.when(source == x)
        def _():
            pbuf[pl.ds(pl.multiple_of(x * 128, 128), 128)] = yq[d - 1]

        @pl.when(source != x)
        def _():
            p_copy(d, x).start()

    def a_copy(q):
        return rcopy(opair.at[1, q - 1, :, 1 - c], cx.at[q - 1], a_send, a_recv.at[q - 1], sib)

    def b_copy(q, d):
        return rcopy(
            qbuf.at[q - 1, (x + d) % 4],
            xrecv.at[d - 1, q - 1],
            b_send.at[d - 1],
            b_recv.at[d - 1, q - 1],
            xdev[d - 1],
        )

    def stage_b(q):
        a_copy(q).wait_recv()
        qbuf[q - 1] = opair[1, q - 1, :, c] + cx[q - 1]
        for d in (1, 3, 2):
            b_copy(q, d).start()

    def stage_f(q):
        for d in (1, 2, 3):
            b_copy(q, d).wait_recv()
        value = (qbuf[q - 1, x] + xrecv[0, q - 1]) + (xrecv[1, q - 1] + xrecv[2, q - 1])
        p = pair_of(q)
        out_ref[:, pl.ds(pl.multiple_of(p * PW, PW), PW)] = value

    th, tl = split(t_ref[...])
    ab_hi[0] = th
    ab_lo[0] = tl
    for a in range(0, SC, 256):
        sh, sl = split(s_ref[:, a : a + 256].T)
        st_hi[a : a + 256] = sh
        st_lo[a : a + 256] = sl
    pl.semaphore_wait(barrier, 12)
    for d in (1, 3, 2):
        y_copy(d).start()

    rs_start(0)
    products_at(0, 3)
    rs_step(0, 2, True)

    @pl.loop(3, 9)
    def _(s):
        @pl.when(s < 8)
        def _():
            products_at(0, s + 1)

        rs_step(0, s)

        @pl.when(s == 3)
        def _():
            forward(1)
            forward(3)

        @pl.when(s == 5)
        def _():
            forward(2)

    rs_final(0)
    ag_start(0)

    @pl.when(x == y)
    def _():
        pbuf[...] = s_ref[:, pl.ds(pl.multiple_of(c * TC, TC), TC)]

    @pl.when(x != y)
    def _():
        for e in (1, 2, 3):
            p_copy(1, (x + e) % 4).wait_recv()

    gh, gl = split(pbuf[...])
    ab_hi[1] = gh
    ab_lo[1] = gl
    rs_start(1)

    def both(s, t_last=6, only_main=False):
        ag_arrive(0, s - 1, t_last)
        rs_step(1, s, only_main)
        opair[0, s - 2] = pair_product(0, s - 1)

    products_at(1, 3)
    both(2, 6, True)

    @pl.loop(3, 8)
    def _(s):
        products_at(1, s + 1)
        both(s)

    both(8, 7)
    rs_final(1)

    @pl.loop(1, NZ)
    def _(e):
        zs_copy(e).start()

    ag_start(1)
    ag_arrive(0, 8, 8)
    opair[0, 7] = pair_product(0, 8)

    def finish(q):
        opair[1, q - 1] = scale[0:1] * (opair[0, q - 1] - scale[1:2] * opair[1, q - 1])
        a_copy(q).start()

    @pl.loop(1, 7)
    def _(t):
        ag_arrive(1, t)
        opair[1, t - 1] = pair_product(1, t)

        @pl.when(t == 2)
        def _():
            zs_all().wait_recv()
            total = zstat[0]
            for o in range(1, NZ):
                total = total + zstat[o]
            tstat[j] = total
            for e in range(1, 8):
                ts_copy(e).start()

        @pl.when(t == 3)
        def _():
            ts_all().wait_recv()
            total = tstat[0]
            for o in range(1, 8):
                total = total + tstat[o]
            ystat[y] = total
            for e in (1, 2, 3):
                ys_copy(e).start()

        @pl.when(t == 4)
        def _():
            ys_all().wait_recv()
            total = (ystat[0] + ystat[1]) + (ystat[2] + ystat[3])
            hsic = jnp.sum(total[:, :128], keepdims=True)
            gram_sq = jnp.sum(total[:, 128:], keepdims=True)
            factor = -2.0 * TOKENS * DS / (jnp.sqrt(gram_sq) * tn_ref[0])
            scale[0:1] = jnp.broadcast_to(factor, (1, 128))
            scale[1:2] = jnp.broadcast_to(hsic / gram_sq, (1, 128))
            pl.loop(1, 5)(finish)

        @pl.when(t == 5)
        def _():
            pl.loop(1, 5)(stage_b)
            finish(5)

        @pl.when(t == 6)
        def _():
            finish(6)
            stage_b(5)

    ag_arrive(1, 7, 7)
    opair[1, 6] = pair_product(1, 7)
    finish(7)
    stage_b(6)
    ag_arrive(1, 8, 8)
    opair[1, 7] = pair_product(1, 8)
    finish(8)
    stage_b(7)
    pl.loop(1, 6)(stage_f)
    stage_b(8)
    pl.loop(6, 9)(stage_f)

    for d in (1, 2, 3):
        y_copy(d).wait_send()

        @pl.when((y + 4 - d) % 4 != x)
        def _():
            p_copy(d, x).wait_send()

    for ph in (0, 1):
        for k in range(KS):
            for d in (0, 1):
                sent = rbuf.at[ph, d, pl.ds(0, 8 if main(d, k) else 7), pl.ds(k * KR, KR)]
                rcopy(sent, sent, rs_send.at[ph, d, k], rs_recv.at[ph, d, 0, k], zdev[d]).wait_send()
                rcopy(sent, sent, ag_send.at[ph, d, k], ag_recv.at[ph, d, 0, k], zdev[d]).wait_send()

    zs_all().wait_send()
    ts_all().wait_send()
    ys_all().wait_send()
    rcopy(cx, cx, a_send, a_recv.at[0], sib).wait_send()
    for d in (1, 2, 3):
        rcopy(xrecv.at[d - 1], xrecv.at[d - 1], b_send.at[d - 1], b_recv.at[d - 1, 0], xdev[d - 1]).wait_send()


def body(student, teacher, teacher_norm):
    f32, bf16 = jnp.float32, jnp.bfloat16
    dma = pltpu.SemaphoreType.DMA
    return pl.pallas_call(
        kernel,
        out_shape=jax.ShapeDtypeStruct((OT, SC), f32),
        in_specs=[
            pl.BlockSpec(memory_space=pltpu.VMEM),
            pl.BlockSpec(memory_space=pltpu.VMEM),
            pl.BlockSpec(memory_space=pltpu.SMEM),
        ],
        out_specs=pl.BlockSpec(memory_space=pltpu.VMEM),
        scratch_shapes=[
            pltpu.VMEM((SC, TOK), bf16),
            pltpu.VMEM((SC, TOK), bf16),
            pltpu.VMEM((2, TOK, TC), bf16),
            pltpu.VMEM((2, TOK, TC), bf16),
            pltpu.VMEM((3, 128, TC), f32),
            pltpu.VMEM((TOK, TC), f32),
            pltpu.VMEM((2, SC, TC), f32),
            pltpu.VMEM((2, 2, 8, CH, TC), f32),
            pltpu.VMEM((2, SC, TC), f32),
            pltpu.VMEM((2, NP, 4, 2, OT, PW), f32),
            pltpu.VMEM((NP, 4, OT, PW), f32),
            pltpu.VMEM((NP, 4, OT, PW), f32),
            pltpu.VMEM((3, NP, OT, PW), f32),
            pltpu.VMEM((NZ, 1, 256), f32),
            pltpu.VMEM((8, 1, 256), f32),
            pltpu.VMEM((4, 1, 256), f32),
            pltpu.VMEM((8, 128), f32),
            dma((2, 2, KS)),
            dma((2, 2, 8, KS)),
            dma((2, 2, KS)),
            dma((2, 2, 8, KS)),
            dma((3,)),
            dma((3,)),
            dma((3,)),
            dma((4,)),
            dma,
            dma,
            dma,
            dma,
            dma,
            dma,
            dma,
            dma((8,)),
            dma((3,)),
            dma((3, 8)),
        ],
        compiler_params=pltpu.CompilerParams(
            collective_id=0, has_side_effects=True, vmem_limit_bytes=48 * 1024 * 1024
        ),
    )(student, teacher, teacher_norm)


def solution(mesh):
    return jax.shard_map(
        body,
        mesh=mesh,
        in_specs=(P("tok", "scol"), P("tok", "tcol"), P()),
        out_specs=P(("tok", "tcol"), "scol"),
        check_vma=False,
    )
```

time: 146 us -> 132 us (0.904)
  Pallas kernels: 142 us -> 128 us
    pallas_call x1, Pallas kernels: 142 us -> 128 us  [body(): pl.pallas_call(kernel, out_shape=jax.ShapeDtypeStruct((OT, SC), f32), in_...]
where the time goes in v2:
time: 132 us
  Pallas kernels  128 us (97%)
  local copies, waits for them, and re-layouts  3.51 us (3%)
    pallas_call x1, Pallas kernels, body(): pl.pallas_call(kernel, out_shape=jax.ShapeDtypeStruct((OT, SC), f32), in_...  128 us
    unnamed x5, local copies, waits for them, and re-layouts  3.51 us

profile of v2, /device:TPU:1, one launch (start us, length us, event | category | flops | bytes accessed | tf_op | source)
XLA Modules:
  0.0 132.1 jit_solution(9439227460254877815)
XLA Ops:
  0.7 0.0 copy-start
  0.7 1.6 %copy-done = f32[512,1024]{1,0:T(8,128)S(1)} copy-done((f32[512,1024]{1,0:T(8,128)S(1)}, f32[512,1024]{1,0:T(8,128)}, u32[]{:S(2)}) %copy-start) | copy-done | bytes 2097176
  2.2 0.0 copy-start.1
  2.2 1.2 copy-done.1
  3.5 127.9 %shard_map.37 = f32[64,1024]{1,0:T(8,128)S(1)} custom-call(f32[512,1024]{1,0:T(8,128)S(1)} %copy-done, f32[512,512]{1,0:T(8,128)S(1)} %copy-done.1, f32[1]{0:T(128)S(6)} %copy.5.tn_ref), custom_call_target="tpu_custom_call" | custom-call | tf_op jit(solution)/shard_map/pallas_call | solution.py:467
  131.4 0.7 copy.6
Async XLA Ops:
  0.7 1.6 %copy-start = (f32[512,1024]{1,0:T(8,128)S(1)}, f32[512,1024]{1,0:T(8,128)}, u32[]{:S(2)}) copy-start(f32[512,1024]{1,0:T(8,128)} %s_ref.1) | copy-start | bytes 6291460
  2.2 1.2 copy-start.1

commit v3 on v2

--- a/solution.py
+++ b/solution.py
@@ -39,6 +39,9 @@
     t_ref,
     tn_ref,
     out_ref,
+    sbuf,
+    tbuf,
+    load_sem,
     st_hi,
     st_lo,
     ab_hi,
@@ -140,10 +143,11 @@
         )
 
     def rs_start(ph):
-        products(ph, (z + 8) % NZ, z)
         for k in range(KS):
             rs_first(ph, 0 if k < KS // 2 else 1, k).start()
-        products_at(ph, 2)
+        if ph == 0:
+            prepare(2)
+        products(ph, 2)
         for k in range(KS):
             rs_second(ph, 1 if k < KS // 2 else 0, k).start()
 
@@ -171,7 +175,15 @@
             for a in range(0, KR, 8):
                 for b in range(0, TC, 128):
                     total = total + square[a : a + 8, b : b + 128]
+            if k < KS - 1:
+                for d in (0, 1):
+                    ag_copy(ph, d, 1, k).start()
         zstat[z, :, ph * 128 : ph * 128 + 128] = jnp.sum(total, axis=0, keepdims=True)
+        if ph == 1:
+            for e in range(1, NZ):
+                zs_copy(e).start()
+        for d in (0, 1):
+            ag_copy(ph, d, 1, KS - 1).start()
 
     def ag_copy(ph, d, t, k):
         o = (z + NZ + 1 - t) % NZ if d == 0 else (z + t - 1) % NZ
@@ -193,11 +205,6 @@
             zdev[d],
         ).wait_recv()
 
-    def ag_start(ph):
-        for k in range(KS):
-            for d in (0, 1):
-                ag_copy(ph, d, 1, k).start()
-
     def ag_arrive(ph, t, last=6):
         for k in range(KS):
             for d in (0, 1):
@@ -206,17 +213,20 @@
                 if last < 7 or (last == 7 and main(d, k)):
                     ag_copy(ph, d, t + 1, k).start()
 
-    def products(ph, o1, o2):
-        r1 = pl.ds(pl.multiple_of(o1 * CH, CH), CH)
-        r2 = pl.ds(pl.multiple_of(o2 * CH, CH), CH)
-        lh = jnp.concatenate([st_hi[r1], st_hi[r2]], axis=0)
-        ll = jnp.concatenate([st_lo[r1], st_lo[r2]], axis=0)
-        value = dot3(lh, ll, ab_hi[ph], ab_lo[ph], ((1,), (0,)))
-        own[ph, r1] = value[:CH]
-        own[ph, r2] = value[CH:]
-
-    def products_at(ph, s):
-        products(ph, (z + 9 - s) % NZ, (z + s + 7) % NZ)
+    def block_of(s):
+        up = (z + s) % 2
+        p = ((up * (z + 7 + s) + (1 - up) * (z + 9 - s)) % NZ) // 2
+        return pl.ds(pl.multiple_of(p * PW, PW), PW)
+
+    def prepare(s):
+        at = block_of(s)
+        sh, sl = split(sbuf[:, at].T)
+        st_hi[at] = sh
+        st_lo[at] = sl
+
+    def products(ph, s):
+        at = block_of(s)
+        own[ph, at] = dot3(st_hi[at], st_lo[at], ab_hi[ph], ab_lo[ph], ((1,), (0,)))
 
     def pair_of(t):
         up = (z + t) % 2
@@ -225,7 +235,12 @@
     def pair_product(ph, t):
         p = pair_of(t)
         wh, wl = split(full[ph, pl.ds(pl.multiple_of(p * PW, PW), PW)])
-        value = dot3(ab_hi[ph], ab_lo[ph], wh, wl, ((1,), (1,)))
+
+        def one(a, b):
+            return lax.dot_general(a, b, (((1,), (1,)), ((), ())), preferred_element_type=jnp.float32)
+
+        wide = one(ab_hi[ph], jnp.concatenate([wh, wl], axis=0))
+        value = wide[:, :PW] + (wide[:, PW:] + one(ab_lo[ph], wh))
         return value.reshape(4, 2, OT, PW)
 
     def zs_copy(e):
@@ -251,7 +266,7 @@
 
     def y_copy(d):
         return rcopy(
-            s_ref.at[pl.ds(pl.multiple_of(x * 128, 128), 128), pl.ds(pl.multiple_of(c * TC, TC), TC)],
+            sbuf.at[pl.ds(pl.multiple_of(x * 128, 128), 128), pl.ds(pl.multiple_of(c * TC, TC), TC)],
             yq.at[d - 1],
             y_send.at[d - 1],
             y_recv.at[d - 1],
@@ -304,26 +319,31 @@
         p = pair_of(q)
         out_ref[:, pl.ds(pl.multiple_of(p * PW, PW), PW)] = value
 
-    th, tl = split(t_ref[...])
+    loads = [pltpu.make_async_copy(t_ref, tbuf, load_sem.at[0]), pltpu.make_async_copy(s_ref, sbuf, load_sem.at[1])]
+    for load in loads:
+        load.start()
+    loads[0].wait()
+    th, tl = split(tbuf[...])
     ab_hi[0] = th
     ab_lo[0] = tl
-    for a in range(0, SC, 256):
-        sh, sl = split(s_ref[:, a : a + 256].T)
-        st_hi[a : a + 256] = sh
-        st_lo[a : a + 256] = sl
+    loads[1].wait()
+    prepare(1)
+    products(0, 1)
     pl.semaphore_wait(barrier, 12)
     for d in (1, 3, 2):
         y_copy(d).start()
 
     rs_start(0)
-    products_at(0, 3)
+    prepare(3)
+    products(0, 3)
     rs_step(0, 2, True)
 
     @pl.loop(3, 9)
     def _(s):
         @pl.when(s < 8)
         def _():
-            products_at(0, s + 1)
+            prepare(s + 1)
+            products(0, s + 1)
 
         rs_step(0, s)
 
@@ -337,11 +357,10 @@
             forward(2)
 
     rs_final(0)
-    ag_start(0)
 
     @pl.when(x == y)
     def _():
-        pbuf[...] = s_ref[:, pl.ds(pl.multiple_of(c * TC, TC), TC)]
+        pbuf[...] = sbuf[:, pl.ds(pl.multiple_of(c * TC, TC), TC)]
 
     @pl.when(x != y)
     def _():
@@ -351,6 +370,7 @@
     gh, gl = split(pbuf[...])
     ab_hi[1] = gh
     ab_lo[1] = gl
+    products(1, 1)
     rs_start(1)
 
     def both(s, t_last=6, only_main=False):
@@ -358,30 +378,27 @@
         rs_step(1, s, only_main)
         opair[0, s - 2] = pair_product(0, s - 1)
 
-    products_at(1, 3)
+    products(1, 3)
     both(2, 6, True)
 
     @pl.loop(3, 8)
     def _(s):
-        products_at(1, s + 1)
+        products(1, s + 1)
         both(s)
 
     both(8, 7)
     rs_final(1)
-
-    @pl.loop(1, NZ)
-    def _(e):
-        zs_copy(e).start()
-
-    ag_start(1)
     ag_arrive(0, 8, 8)
     opair[0, 7] = pair_product(0, 8)
 
+    def finish_with(q, second):
+        opair[1, q - 1] = scale[0:1] * (opair[0, q - 1] - scale[1:2] * second)
+        a_copy(q).start()
+
     def finish(q):
-        opair[1, q - 1] = scale[0:1] * (opair[0, q - 1] - scale[1:2] * opair[1, q - 1])
-        a_copy(q).start()
-
-    @pl.loop(1, 7)
+        finish_with(q, opair[1, q - 1])
+
+    @pl.loop(1, 5)
     def _(t):
         ag_arrive(1, t)
         opair[1, t - 1] = pair_product(1, t)
@@ -417,45 +434,42 @@
             scale[1:2] = jnp.broadcast_to(hsic / gram_sq, (1, 128))
             pl.loop(1, 5)(finish)
 
-        @pl.when(t == 5)
-        def _():
-            pl.loop(1, 5)(stage_b)
-            finish(5)
-
-        @pl.when(t == 6)
-        def _():
-            finish(6)
-            stage_b(5)
-
+    ag_arrive(1, 5)
+    finish_with(5, pair_product(1, 5))
+    pl.loop(1, 5)(stage_b)
+    ag_arrive(1, 6)
+    finish_with(6, pair_product(1, 6))
+    stage_b(5)
     ag_arrive(1, 7, 7)
-    opair[1, 6] = pair_product(1, 7)
-    finish(7)
+    finish_with(7, pair_product(1, 7))
     stage_b(6)
     ag_arrive(1, 8, 8)
-    opair[1, 7] = pair_product(1, 8)
-    finish(8)
+    finish_with(8, pair_product(1, 8))
     stage_b(7)
-    pl.loop(1, 6)(stage_f)
-    stage_b(8)
-    pl.loop(6, 9)(stage_f)
-
-    for d in (1, 2, 3):
-        y_copy(d).wait_send()
-
-        @pl.when((y + 4 - d) % 4 != x)
-        def _():
-            p_copy(d, x).wait_send()
-
-    for ph in (0, 1):
+
+    def ring_sent(ph, send, recv):
         for k in range(KS):
             for d in (0, 1):
                 sent = rbuf.at[ph, d, pl.ds(0, 8 if main(d, k) else 7), pl.ds(k * KR, KR)]
-                rcopy(sent, sent, rs_send.at[ph, d, k], rs_recv.at[ph, d, 0, k], zdev[d]).wait_send()
-                rcopy(sent, sent, ag_send.at[ph, d, k], ag_recv.at[ph, d, 0, k], zdev[d]).wait_send()
+                rcopy(sent, sent, send.at[ph, d, k], recv.at[ph, d, 0, k], zdev[d]).wait_send()
+
+    ring_sent(0, rs_send, rs_recv)
+    ring_sent(1, rs_send, rs_recv)
+    pl.loop(1, 6)(stage_f)
+    stage_b(8)
+    ring_sent(0, ag_send, ag_recv)
+    ring_sent(1, ag_send, ag_recv)
+    for d in (1, 2, 3):
+        y_copy(d).wait_send()
+
+        @pl.when((y + 4 - d) % 4 != x)
+        def _():
+            p_copy(d, x).wait_send()
 
     zs_all().wait_send()
     ts_all().wait_send()
     ys_all().wait_send()
+    pl.loop(6, 9)(stage_f)
     rcopy(cx, cx, a_send, a_recv.at[0], sib).wait_send()
     for d in (1, 2, 3):
         rcopy(xrecv.at[d - 1], xrecv.at[d - 1], b_send.at[d - 1], b_recv.at[d - 1, 0], xdev[d - 1]).wait_send()
@@ -468,12 +482,15 @@
         kernel,
         out_shape=jax.ShapeDtypeStruct((OT, SC), f32),
         in_specs=[
-            pl.BlockSpec(memory_space=pltpu.VMEM),
-            pl.BlockSpec(memory_space=pltpu.VMEM),
+            pl.BlockSpec(memory_space=pl.ANY),
+            pl.BlockSpec(memory_space=pl.ANY),
             pl.BlockSpec(memory_space=pltpu.SMEM),
         ],
         out_specs=pl.BlockSpec(memory_space=pltpu.VMEM),
         scratch_shapes=[
+            pltpu.VMEM((TOK, SC), f32),
+            pltpu.VMEM((TOK, TC), f32),
+            dma((2,)),
             pltpu.VMEM((SC, TOK), bf16),
             pltpu.VMEM((SC, TOK), bf16),
             pltpu.VMEM((2, TOK, TC), bf16),
@@ -511,7 +528,7 @@
             dma((3, 8)),
         ],
         compiler_params=pltpu.CompilerParams(
-            collective_id=0, has_side_effects=True, vmem_limit_bytes=48 * 1024 * 1024
+            collective_id=0, has_side_effects=True
         ),
     )(student, teacher, teacher_norm)
 

time: 132 us -> 127 us (0.962)
  Pallas kernels: 128 us -> 125 us
  local copies, waits for them, and re-layouts: 3.51 us -> 1.67 us
    pallas_call x1, Pallas kernels: 128 us -> 125 us  [body(): pl.pallas_call(kernel, out_shape=jax.ShapeDtypeStruct((OT, SC), f32), in_...]
    unnamed x5 -> x1, local copies, waits for them, and re-layouts: 3.51 us -> 1.67 us
where the time goes in v3:
time: 127 us
  Pallas kernels  125 us (98%)
  local copies, waits for them, and re-layouts  1.67 us (1%)
    pallas_call x1, Pallas kernels, body(): pl.pallas_call(kernel, out_shape=jax.ShapeDtypeStruct((OT, SC), f32), in_...  125 us

profile of v3, /device:TPU:1, one launch (start us, length us, event | category | flops | bytes accessed | tf_op | source)
XLA Modules:
  0.0 127.1 jit_solution(4548254013336730354)
XLA Ops:
  0.7 124.8 %shard_map.37 = f32[64,1024]{1,0:T(8,128)} custom-call(f32[512,1024]{1,0:T(8,128)} %s_ref.1, f32[512,512]{1,0:T(8,128)} %t_ref.1, f32[1]{0:T(128)S(6)} %copy.5.tn_ref), custom_call_target="tpu_custom_call" | custom-call | tf_op jit(solution)/shard_map/pallas_call | solution.py:481
  125.5 1.7 %copy.6 = f32[64,1024]{1,0:T(8,128)} copy(f32[64,1024]{1,0:T(8,128)} %shard_map.37) | data formatting | bytes 524288

commit v4 on v3

--- a/solution.py
+++ b/solution.py
@@ -432,17 +432,19 @@
             factor = -2.0 * TOKENS * DS / (jnp.sqrt(gram_sq) * tn_ref[0])
             scale[0:1] = jnp.broadcast_to(factor, (1, 128))
             scale[1:2] = jnp.broadcast_to(hsic / gram_sq, (1, 128))
-            pl.loop(1, 5)(finish)
+            pl.loop(1, 3)(finish)
 
     ag_arrive(1, 5)
-    finish_with(5, pair_product(1, 5))
-    pl.loop(1, 5)(stage_b)
+    opair[1, 4] = pair_product(1, 5)
+    pl.loop(3, 5)(finish)
+    pl.loop(1, 3)(stage_b)
     ag_arrive(1, 6)
     finish_with(6, pair_product(1, 6))
-    stage_b(5)
+    finish(5)
+    pl.loop(3, 5)(stage_b)
     ag_arrive(1, 7, 7)
     finish_with(7, pair_product(1, 7))
-    stage_b(6)
+    pl.loop(5, 7)(stage_b)
     ag_arrive(1, 8, 8)
     finish_with(8, pair_product(1, 8))
     stage_b(7)
@@ -482,8 +484,8 @@
         kernel,
         out_shape=jax.ShapeDtypeStruct((OT, SC), f32),
         in_specs=[
-            pl.BlockSpec(memory_space=pl.ANY),
-            pl.BlockSpec(memory_space=pl.ANY),
+            pl.BlockSpec(memory_space=pltpu.HBM),
+            pl.BlockSpec(memory_space=pltpu.HBM),
             pl.BlockSpec(memory_space=pltpu.SMEM),
         ],
         out_specs=pl.BlockSpec(memory_space=pltpu.VMEM),
@@ -528,7 +530,7 @@
             dma((3, 8)),
         ],
         compiler_params=pltpu.CompilerParams(
-            collective_id=0, has_side_effects=True
+            collective_id=0, has_side_effects=True, vmem_limit_bytes=55_750_000
         ),
     )(student, teacher, teacher_norm)
 

time: 127 us -> 125 us (0.984)
  no operation moved by 1% of the time
where the time goes in v4:
time: 125 us
  Pallas kernels  124 us (99%)
    pallas_call x1, Pallas kernels, body(): pl.pallas_call(kernel, out_shape=jax.ShapeDtypeStruct((OT, SC), f32), in_...  124 us

profile of v4, /device:TPU:1, one launch (start us, length us, event | category | flops | bytes accessed | tf_op | source)
XLA Modules:
  0.0 125.3 jit_solution(3694372434509368122)
XLA Ops:
  0.7 123.9 %shard_map.37 = f32[64,1024]{1,0:T(8,128)S(1)} custom-call(f32[512,1024]{1,0:T(8,128)} %s_ref.1, f32[512,512]{1,0:T(8,128)} %t_ref.1, f32[1]{0:T(128)S(6)} %copy.5.tn_ref), custom_call_target="tpu_custom_call" | custom-call | tf_op jit(solution)/shard_map/pallas_call | solution.py:483
  124.6 0.7 copy.6

commit v5 on v4

--- a/solution.py
+++ b/solution.py
@@ -77,6 +77,9 @@
     a_recv,
     b_send,
     b_recv,
+    last,
+    e_send,
+    e_recv,
 ):
     z = lax.axis_index("tok")
     y = lax.axis_index("scol")
@@ -179,11 +182,11 @@
                 for d in (0, 1):
                     ag_copy(ph, d, 1, k).start()
         zstat[z, :, ph * 128 : ph * 128 + 128] = jnp.sum(total, axis=0, keepdims=True)
+        for d in (0, 1):
+            ag_copy(ph, d, 1, KS - 1).start()
         if ph == 1:
             for e in range(1, NZ):
                 zs_copy(e).start()
-        for d in (0, 1):
-            ag_copy(ph, d, 1, KS - 1).start()
 
     def ag_copy(ph, d, t, k):
         o = (z + NZ + 1 - t) % NZ if d == 0 else (z + t - 1) % NZ
@@ -305,6 +308,14 @@
             b_recv.at[d - 1, q - 1],
             xdev[d - 1],
         )
+
+    def e_copy(e):
+        o = (j + e) % 8
+        return rcopy(opair.at[1, NP - 1, o // 2, o % 2], last.at[j], e_send, e_recv, tdev[e - 1])
+
+    def e_all():
+        part = last.at[pl.ds(0, 7)]
+        return rcopy(part, part, e_send, e_recv, tdev[0])
 
     def stage_b(q):
         a_copy(q).wait_recv()
@@ -446,7 +457,9 @@
     finish_with(7, pair_product(1, 7))
     pl.loop(5, 7)(stage_b)
     ag_arrive(1, 8, 8)
-    finish_with(8, pair_product(1, 8))
+    opair[1, 7] = scale[0:1] * (opair[0, 7] - scale[1:2] * pair_product(1, 8))
+    for e in (2, 6, 3, 5, 4, 7, 1):
+        e_copy(e).start()
     stage_b(7)
 
     def ring_sent(ph, send, recv):
@@ -458,7 +471,6 @@
     ring_sent(0, rs_send, rs_recv)
     ring_sent(1, rs_send, rs_recv)
     pl.loop(1, 6)(stage_f)
-    stage_b(8)
     ring_sent(0, ag_send, ag_recv)
     ring_sent(1, ag_send, ag_recv)
     for d in (1, 2, 3):
@@ -471,10 +483,18 @@
     zs_all().wait_send()
     ts_all().wait_send()
     ys_all().wait_send()
-    pl.loop(6, 9)(stage_f)
-    rcopy(cx, cx, a_send, a_recv.at[0], sib).wait_send()
+    pl.loop(6, 8)(stage_f)
+    e_all().wait_recv()
+    value = opair[1, 7, x, c]
+    for e in range(1, 8):
+        value = value + last[(j + e) % 8]
+    out_ref[:, pl.ds(pl.multiple_of(pair_of(8) * PW, PW), PW)] = value
+    e_all().wait_send()
+    done = cx.at[pl.ds(0, 7)]
+    rcopy(done, done, a_send, a_recv.at[0], sib).wait_send()
     for d in (1, 2, 3):
-        rcopy(xrecv.at[d - 1], xrecv.at[d - 1], b_send.at[d - 1], b_recv.at[d - 1, 0], xdev[d - 1]).wait_send()
+        done = xrecv.at[d - 1, pl.ds(0, 7)]
+        rcopy(done, done, b_send.at[d - 1], b_recv.at[d - 1, 0], xdev[d - 1]).wait_send()
 
 
 def body(student, teacher, teacher_norm):
@@ -528,6 +548,9 @@
             dma((8,)),
             dma((3,)),
             dma((3, 8)),
+            pltpu.VMEM((8, OT, PW), f32),
+            dma,
+            dma,
         ],
         compiler_params=pltpu.CompilerParams(
             collective_id=0, has_side_effects=True, vmem_limit_bytes=55_750_000

time: 125 us -> 125 us (level)
  no operation moved by 1% of the time
where the time goes in v5:
time: 125 us
  Pallas kernels  124 us (99%)
    pallas_call x1, Pallas kernels, body(): pl.pallas_call(kernel, out_shape=jax.ShapeDtypeStruct((OT, SC), f32), in_...  124 us

profile of v5, /device:TPU:1, one launch (start us, length us, event | category | flops | bytes accessed | tf_op | source)
XLA Modules:
  0.0 124.9 jit_solution(12588922411654191185)
XLA Ops:
  0.7 123.5 %shard_map.37 = f32[64,1024]{1,0:T(8,128)S(1)} custom-call(f32[512,1024]{1,0:T(8,128)} %s_ref.1, f32[512,512]{1,0:T(8,128)} %t_ref.1, f32[1]{0:T(128)S(6)} %copy.5.tn_ref), custom_call_target="tpu_custom_call" | custom-call | tf_op jit(solution)/shard_map/pallas_call | solution.py:503
  124.2 0.7 copy.6
